TPU v7x, 32 devices: a whole 2x2x4 slice. The times are simulated.
32 devices in a mesh: lat: 8 (over y, x, core), lon: 4 (over z).
Axes of the slice: x: 2, y: 2, z: 4, core: 2. Of those that a mesh axis runs over, the one named last changes fastest.
Arguments:
- snapshots: float32 [1024, 128, 512], P(None, 'lat', 'lon'), may hold values from -60 to 60
- land_sea: int32 [128, 512], P('lat', 'lon'), may hold values 0 or 1
- penalty: float32 [128, 512], P('lat', 'lon'), may hold values from 0.003 to 0.03
- initial_basis: float32 [64, 128, 512], P(None, 'lat', 'lon'), may hold values from -6 to 6
Outputs:
- leading_basis: float32 [64, 128, 512], P(None, 'lat', 'lon')
- rayleigh_matrix: float32 [64, 64], replicated
All inputs are finite; a program needn't handle non-finite values. No bound on the sum of `land_sea` on one device may be relied on, other than what follows from the above.
Results may differ from a plain program's by a relative error of at most 0.0003.
Values sent between devices are 32-bit elements; how exact they have to be, the bound alone decides.
A program may use at most 64 MiB of HBM per device.

v0:
```python
import jax
import jax.numpy as jnp
from jax import lax
from jax.sharding import PartitionSpec as P

STEPS = 2


def padded_2(block, sides, width):
    for axis, dim in sides:
        count = lax.axis_size(axis)
        forward = [(i, i + 1) for i in range(count - 1)]
        backward = [(target, source) for source, target in forward]
        low = lax.ppermute(
            lax.slice_in_dim(block, block.shape[dim] - width, None, axis=dim), axis, forward
        )
        high = lax.ppermute(lax.slice_in_dim(block, 0, width, axis=dim), axis, backward)
        block = jnp.concatenate([low, block, high], axis=dim)
    return block


def laplacian(masked_field):
    padded = padded_2(masked_field, (("lat", 1), ("lon", 2)), 1)
    neighbours = (
        padded[:, 2:, 1:-1] + padded[:, :-2, 1:-1] + padded[:, 1:-1, 2:] + padded[:, 1:-1, :-2]
    )
    return neighbours - 4.0 * masked_field


def project_points(snapshots, masked_field):
    return jnp.einsum("tab,kab->tk", snapshots, masked_field, precision=lax.Precision.HIGHEST)


def expand_points(snapshots, coeffs):
    return jnp.einsum("tab,tk->kab", snapshots, coeffs, precision=lax.Precision.HIGHEST)


def inner_products(left_field, right_field):
    return jnp.einsum("kab,jab->kj", left_field, right_field, precision=lax.Precision.HIGHEST)


def apply_inverse(factor, stacked):
    solved = jax.scipy.linalg.solve_triangular(
        factor, stacked.reshape(stacked.shape[0], -1), lower=True
    )
    return solved.reshape(stacked.shape)


def total_terms(term_tuple):
    shares = (lax.psum_scatter(term_tuple[0], "lat", scatter_dimension=0, tiled=True),)
    summed = lax.psum((shares[0],), "lon")
    return (lax.all_gather(summed[0], "lat", axis=0, tiled=True),)


def local(snapshots, land_sea, penalty, initial_basis):
    ocean_mask = land_sea.astype(jnp.float32)
    point_count = float(
        snapshots.shape[1] * snapshots.shape[2] * lax.axis_size("lat") * lax.axis_size("lon")
    )
    current_basis = initial_basis * ocean_mask
    for iteration in range(STEPS):
        (coeffs,) = total_terms((project_points(snapshots, current_basis),))
        applied = ocean_mask * (
            expand_points(snapshots, coeffs) / point_count + penalty * laplacian(current_basis)
        )
        (moments,) = total_terms((inner_products(applied, applied),))
        factor = jnp.linalg.cholesky(moments / point_count)
        current_basis = apply_inverse(factor, applied)
    (coeffs,) = total_terms((project_points(snapshots, current_basis),))
    smoothed = laplacian(current_basis)
    final_image = ocean_mask * (expand_points(snapshots, coeffs) / point_count + penalty * smoothed)
    (projected,) = total_terms((inner_products(current_basis, final_image),))
    return (current_basis, projected / point_count)


def solution(mesh):
    in_specs = (P(None, "lat", "lon"), P("lat", "lon"), P("lat", "lon"), P(None, "lat", "lon"))
    out_specs = (P(None, "lat", "lon"), P())
    return jax.shard_map(local, mesh=mesh, in_specs=in_specs, out_specs=out_specs, check_vma=False)
```

profile of v0, /device:TPU:0, one launch (start us, length us, event | category | flops | bytes accessed | tf_op | source)
XLA Modules:
  0.0 464.0 jit_solution(17767832957010539441)
XLA Ops:
  7.2 0.7 convert_element_type.3
  7.9 1.2 copy_multiply_fusion
  9.2 1.3 collective-permute-start
  10.5 3.0 collective-permute-start.1
  13.5 12.8 %fusion.39 = f32[1024,64]{0,1:T(8,128)} fusion(f32[64,16,128]{2,0,1:T(8,128)S(1)} %copy_multiply_fusion, f32[1024,16,128]{2,1,0:T(8,128)} %param.7), kind=kOutput, calls=%fused_computation.22 | convolution fusion | flops 1610612736 | bytes 9175040 | tf_op jit(solution)/shard_map/tab,kab->tk/dot_general | solution.py:31
  26.9 1.3 collective-permute-start.2
  28.5 5.6 %collective-permute-start.3 = (f32[64,18,1]{0,2,1:T(1,128)S(1)}, f32[64,18,1]{0,2,1:T(1,128)S(1)}, u32[]{:S(2)}, u32[]{:S(2)}) collective-permute-start(f32[64,18,1]{0,2,1:T(1,128)S(1)} %copy.45), channel_id=1, source_target_pairs={{0,1},{1,2},{2,3},{4,5},{5,6},{6,7},{8,9},{9,10},{10,11},{12,13},{... | collective-permute-start | bytes 13832 | tf_op jit(solution)/shard_map/ppermute | solution.py:14
  34.1 0.6 dynamic-slice
  35.3 0.3 copy.44
  35.6 0.3 copy.46
  35.9 27.7 %reduce-scatter.7.cloned.1.call-done = f32[128,64]{0,1:T(8,128)} async-done(((f32[1024,64]{0,1:T(8,128)}), f32[128,64]{0,1:T(8,128)}) %reduce-scatter.7.cloned.1.call-update) | async-done | bytes 32784 | tf_op jit(solution)/shard_map/reduce_scatter | solution.py:50
  63.6 19.6 %psum.42 = f32[128,64]{0,1:T(8,128)S(1)} all-reduce(f32[128,64]{0,1:T(8,128)} %reduce-scatter.7.cloned.1.call-done), channel_id=1, replica_groups=mesh['lat'=8,'lon'=4] {'lon'}, use_global_device_ids=true, to_apply=%region_1.0 | all-reduce | flops 8192 | bytes 65536 | tf_op jit(solution)/shard_map/psum | solution.py:51
  83.2 9.8 %all_gather.18 = f32[1024,64]{0,1:T(8,128)S(1)} all-gather(f32[128,64]{0,1:T(8,128)S(1)} %psum.42), channel_id=1, replica_groups=mesh['lat'=8,'lon'=4] {'lat'}, dimensions={0}, use_global_device_ids=true | all-gather | bytes 294912 | tf_op jit(solution)/shard_map/all_gather | solution.py:52
  93.0 9.8 %fusion.36 = f32[64,16,128]{2,0,1:T(8,128)S(1)} fusion(f32[1024,16,128]{2,1,0:T(8,128)} %param.7, f32[64,18,1]{2,0,1:T(8,128)S(1)} %copy.46, f32[64,1,128]{2,0,1:T(8,128)S(1)} %collective-permute-done, f32[64,16,128]{2,0,1:T(8,128)S(1)} %copy_multiply_fusion, f32[64,1,128]{2,0,1:T(8,128)S(1)} %collective-permute-done.1, f32[64,18,1]{2,0,1:T(8,128)S(1)} %copy.44, ...), kind=kOutput, calls=%fused_computation.20 | convolution fusion | flops 1612840960 | bytes 9790464 | tf_op jit(solution)/shard_map/tab,tk->kab/dot_general | solution.py:35
  102.8 0.6 convolution_bitcast_fusion.3
  103.4 23.6 %all-reduce = f32[64,64]{0,1:T(8,128)S(1)} all-reduce(f32[64,64]{0,1:T(8,128)S(1)} %convolution_bitcast_fusion.3), channel_id=3, replica_groups=mesh['lat'=8,'lon'=4] {'lat'}, use_global_device_ids=true, to_apply=%region_2.0.clone | all-reduce | flops 4096 | bytes 32768
  127.0 15.8 %psum.43 = f32[8,64]{0,1:T(8,128)S(1)} all-reduce(f32[8,64]{0,1:T(8,128)S(1)} %constant_dynamic-slice_fusion.2), channel_id=1, replica_groups=mesh['lat'=8,'lon'=4] {'lon'}, use_global_device_ids=true, to_apply=%region_3.0 | all-reduce | flops 512 | bytes 4096 | tf_op jit(solution)/shard_map/psum | solution.py:51
  142.9 8.6 %all_gather.19 = f32[64,64]{1,0:T(8,128)S(1)} all-gather(f32[8,64]{1,0:T(8,128)S(1)} %copy.48), channel_id=1, replica_groups=mesh['lat'=8,'lon'=4] {'lat'}, dimensions={0}, use_global_device_ids=true | all-gather | bytes 18432 | tf_op jit(solution)/shard_map/all_gather | solution.py:52
  151.7 5.8 %cholesky.44 = f32[64,64]{1,0:T(8,128)S(1)} custom-call(f32[64,64]{1,0:T(8,128)S(1)} %fusion.76), custom_call_target="Cholesky" | custom-call | tf_op jit(solution)/shard_map/jit(cholesky)/cholesky | solution.py:67
  157.5 0.6 compare_reduce_fusion.1
  158.2 0.7 fusion.71
  158.8 4.9 %custom-call.6 = f32[1,64,64]{1,2,0:T(8,128)S(1)} custom-call(f32[1,64,64]{2,1,0:T(8,128)S(1)} %fusion.71), custom_call_target="InvertDiagBlocksLowerTriangular" | custom-call | tf_op jit(solution)/shard_map/jit(_solve_triangular)/triangular_solve | solution.py:43
  163.7 0.6 convolution_bitcast_fusion
  164.5 2.3 collective-permute-start.5
  166.7 12.8 %fusion.42 = f32[1024,64]{0,1:T(8,128)} fusion(f32[1024,16,128]{2,1,0:T(8,128)} %param.7, f32[8,16,8,128]{3,2,1,0:T(8,128)S(1)} %convolution_bitcast_fusion), kind=kOutput, calls=%fused_computation.23 | convolution fusion | flops 1610612736 | bytes 9175040 | tf_op jit(solution)/shard_map/tab,kab->tk/dot_general | solution.py:31
  179.6 1.3 collective-permute-start.4
  181.0 2.4 collective-permute-done.4
  183.8 1.3 collective-permute-start.6
  185.4 4.6 collective-permute-start.7
  189.9 0.3 copy.61
  190.2 1.1 collective-permute-done.7
  191.3 0.3 copy.63
  191.5 24.7 %reduce-scatter.9.cloned.1.call-done = f32[128,64]{0,1:T(8,128)} async-done(((f32[1024,64]{0,1:T(8,128)}), f32[128,64]{0,1:T(8,128)}) %reduce-scatter.9.cloned.1.call-update) | async-done | bytes 32784 | tf_op jit(solution)/shard_map/reduce_scatter | solution.py:50
  216.3 19.6 %psum.44 = f32[128,64]{0,1:T(8,128)S(1)} all-reduce(f32[128,64]{0,1:T(8,128)} %reduce-scatter.9.cloned.1.call-done), channel_id=1, replica_groups=mesh['lat'=8,'lon'=4] {'lon'}, use_global_device_ids=true, to_apply=%region_7.0 | all-reduce | flops 8192 | bytes 65536 | tf_op jit(solution)/shard_map/psum | solution.py:51
  235.9 10.0 %all_gather.20 = f32[1024,64]{0,1:T(8,128)S(1)} all-gather(f32[128,64]{0,1:T(8,128)S(1)} %psum.44), channel_id=1, replica_groups=mesh['lat'=8,'lon'=4] {'lat'}, dimensions={0}, use_global_device_ids=true | all-gather | bytes 294912 | tf_op jit(solution)/shard_map/all_gather | solution.py:52
  245.9 9.8 %fusion.33 = f32[64,16,128]{2,0,1:T(8,128)S(1)} fusion(f32[1024,16,128]{2,1,0:T(8,128)} %param.7, f32[64,18,128]{2,0,1:T(8,128)S(1)} %constant_dynamic-update-slice_fusion, f32[64,18,1]{2,0,1:T(8,128)S(1)} %copy.63, f32[64,18,1]{2,0,1:T(8,128)S(1)} %copy.61, f32[64,16,128]{2,0,1:T(8,128)S(1)} %bitcast.101, f32[64,1,128]{2,0,1:T(8,128)S(1)} %collective-permute-done.5, ...), kind=kOutput, calls=%fused_computation.19 | convolution fusion | flops 1612316672 | bytes 10380288 | tf_op jit(solution)/shard_map/tab,tk->kab/dot_general | solution.py:35
  255.7 0.6 convolution_bitcast_fusion.2
  256.3 23.6 %all-reduce.1 = f32[64,64]{0,1:T(8,128)S(1)} all-reduce(f32[64,64]{0,1:T(8,128)S(1)} %convolution_bitcast_fusion.2), channel_id=5, replica_groups=mesh['lat'=8,'lon'=4] {'lat'}, use_global_device_ids=true, to_apply=%region_8.0.clone | all-reduce | flops 4096 | bytes 32768
  280.0 15.8 %psum.45 = f32[8,64]{0,1:T(8,128)S(1)} all-reduce(f32[8,64]{0,1:T(8,128)S(1)} %constant_dynamic-slice_fusion.1), channel_id=1, replica_groups=mesh['lat'=8,'lon'=4] {'lon'}, use_global_device_ids=true, to_apply=%region_9.0 | all-reduce | flops 512 | bytes 4096 | tf_op jit(solution)/shard_map/psum | solution.py:51
  295.8 8.1 %all_gather.21 = f32[64,64]{1,0:T(8,128)S(1)} all-gather(f32[8,64]{1,0:T(8,128)S(1)} %copy.66), channel_id=1, replica_groups=mesh['lat'=8,'lon'=4] {'lat'}, dimensions={0}, use_global_device_ids=true | all-gather | bytes 18432 | tf_op jit(solution)/shard_map/all_gather | solution.py:52
  304.1 5.8 %cholesky.55 = f32[64,64]{1,0:T(8,128)S(1)} custom-call(f32[64,64]{1,0:T(8,128)S(1)} %fusion.74), custom_call_target="Cholesky" | custom-call | tf_op jit(solution)/shard_map/jit(cholesky)/cholesky | solution.py:67
  310.0 0.6 compare_reduce_fusion
  310.6 0.7 fusion.72
  311.3 4.9 %custom-call.7 = f32[1,64,64]{1,2,0:T(8,128)S(1)} custom-call(f32[1,64,64]{2,1,0:T(8,128)S(1)} %fusion.72), custom_call_target="InvertDiagBlocksLowerTriangular" | custom-call | tf_op jit(solution)/shard_map/jit(_solve_triangular)/triangular_solve | solution.py:43
  316.2 0.6 fusion.48
  316.9 2.3 collective-permute-start.9
  319.2 12.8 %fusion.45 = f32[1024,64]{0,1:T(8,128)} fusion(f32[1024,16,128]{2,1,0:T(8,128)} %param.7, f32[64,2048]{1,0:T(8,128)S(1)} %fusion.48), kind=kOutput, calls=%fused_computation.24 | convolution fusion | flops 1610612736 | bytes 9175040 | tf_op jit(solution)/shard_map/tab,kab->tk/dot_general | solution.py:31
  332.0 1.5 collective-permute-start.8
  333.6 2.2 collective-permute-done.8
  336.1 0.2 copy.78
  336.3 1.3 collective-permute-start.10
  337.8 4.6 collective-permute-start.11
  342.4 0.9 copy.104
  343.3 0.3 copy.79
  343.7 0.3 copy.81
  344.0 24.9 %reduce-scatter.11.cloned.1.call-done = f32[128,64]{0,1:T(8,128)} async-done(((f32[1024,64]{0,1:T(8,128)}), f32[128,64]{0,1:T(8,128)}) %reduce-scatter.11.cloned.1.call-update) | async-done | bytes 32784 | tf_op jit(solution)/shard_map/reduce_scatter | solution.py:50
  368.9 19.6 %psum.46 = f32[128,64]{0,1:T(8,128)S(1)} all-reduce(f32[128,64]{0,1:T(8,128)} %reduce-scatter.11.cloned.1.call-done), channel_id=1, replica_groups=mesh['lat'=8,'lon'=4] {'lon'}, use_global_device_ids=true, to_apply=%region_11.0 | all-reduce | flops 8192 | bytes 65536 | tf_op jit(solution)/shard_map/psum | solution.py:51
  388.5 9.8 %all_gather.22 = f32[1024,64]{0,1:T(8,128)S(1)} all-gather(f32[128,64]{0,1:T(8,128)S(1)} %psum.46), channel_id=1, replica_groups=mesh['lat'=8,'lon'=4] {'lat'}, dimensions={0}, use_global_device_ids=true | all-gather | bytes 294912 | tf_op jit(solution)/shard_map/all_gather | solution.py:52
  398.4 9.8 %fusion.30 = f32[64,16,128]{2,0,1:T(8,128)S(1)} fusion(f32[1024,16,128]{2,1,0:T(8,128)} %param.7, f32[64,18,128]{2,0,1:T(8,128)S(1)} %constant_dynamic-update-slice_fusion.3, f32[64,18,1]{2,0,1:T(8,128)S(1)} %copy.81, f32[64,18,1]{2,0,1:T(8,128)S(1)} %copy.79, f32[64,16,128]{2,0,1:T(8,128)S(1)} %copy_bitcast_fusion, ...), kind=kOutput, calls=%fused_computation.18 | convolution fusion | flops 1612316672 | bytes 10380288 | tf_op jit(solution)/shard_map/tab,tk->kab/dot_general | solution.py:35
  408.2 0.6 convolution_bitcast_fusion.1
  408.8 23.6 %all-reduce.2 = f32[64,64]{0,1:T(8,128)S(1)} all-reduce(f32[64,64]{0,1:T(8,128)S(1)} %convolution_bitcast_fusion.1), channel_id=7, replica_groups=mesh['lat'=8,'lon'=4] {'lat'}, use_global_device_ids=true, to_apply=%region_12.15.clone | all-reduce | flops 4096 | bytes 32768
  432.5 15.8 %psum.47 = f32[8,64]{0,1:T(8,128)S(1)} all-reduce(f32[8,64]{0,1:T(8,128)S(1)} %constant_dynamic-slice_fusion), channel_id=1, replica_groups=mesh['lat'=8,'lon'=4] {'lon'}, use_global_device_ids=true, to_apply=%region_13.16 | all-reduce | flops 512 | bytes 4096 | tf_op jit(solution)/shard_map/psum | solution.py:51
  448.3 8.1 %all_gather.23 = f32[64,64]{1,0:T(8,128)S(1)} all-gather(f32[8,64]{1,0:T(8,128)S(1)} %copy.85), channel_id=1, replica_groups=mesh['lat'=8,'lon'=4] {'lat'}, dimensions={0}, use_global_device_ids=true | all-gather | bytes 18432 | tf_op jit(solution)/shard_map/all_gather | solution.py:52
  456.5 0.7 copy.87
  (57 shorter events, 3.3 us)
Async XLA Ops:
  7.2 26.9 %copy-start.1 = (u32[32]{0:T(128)S(1)}, u32[32]{0:T(128)}, u32[]{:S(2)}) copy-start(u32[32]{0:T(128)} %constant.44) | copy-start | bytes 388
  7.2 56.4 %reduce-scatter.7.cloned.1.call-start = ((), (), s32[]{:S(2)}) async-start(), calls=%async_computation.3 | async-start | bytes 294912 | tf_op jit(solution)/shard_map/reduce_scatter | solution.py:50
  7.9 85.1 %copy-start = (f32[16,128]{1,0:T(8,128)S(1)}, f32[16,128]{1,0:T(8,128)}, u32[]{:S(2)}) copy-start(f32[16,128]{1,0:T(8,128)} %param.9) | copy-start | bytes 24580
  9.2 17.2 %collective-permute-start = (f32[64,1,128]{2,0,1:T(8,128)S(1)}, f32[64,1,128]{2,0,1:T(8,128)S(1)}, u32[]{:S(2)}, u32[]{:S(2)}) collective-permute-start(f32[64,1,128]{2,0,1:T(8,128)S(1)} %get-tuple-element.21), channel_id=1, source_target_pairs={{4,0},{8,4},{12,8},{16,12},{20,16},{24,20},{28,24},{5,1},{9,5},{13... | collective-permute-start | bytes 98312 | tf_op jit(solution)/shard_map/ppermute | solution.py:17
  10.5 16.0 %collective-permute-start.1 = (f32[64,1,128]{2,0,1:T(8,128)S(1)}, f32[64,1,128]{2,0,1:T(8,128)S(1)}, u32[]{:S(2)}, u32[]{:S(2)}) collective-permute-start(f32[64,1,128]{2,0,1:T(8,128)S(1)} %get-tuple-element.20), channel_id=1, source_target_pairs={{0,4},{4,8},{8,12},{12,16},{16,20},{20,24},{24,28},{1,5},{5,9},{9,... | collective-permute-start | bytes 98312 | tf_op jit(solution)/shard_map/ppermute | solution.py:14
  26.4 189.9 %reduce-scatter.9.cloned.1.call-start = ((), (), s32[]{:S(2)}) async-start(), calls=%async_computation.4 | async-start | bytes 294912 | tf_op jit(solution)/shard_map/reduce_scatter | solution.py:50
  26.9 8.4 %collective-permute-start.2 = (f32[64,18,1]{0,2,1:T(1,128)S(1)}, f32[64,18,1]{0,2,1:T(1,128)S(1)}, u32[]{:S(2)}, u32[]{:S(2)}) collective-permute-start(f32[64,18,1]{0,2,1:T(1,128)S(1)} %copy.43), channel_id=1, source_target_pairs={{1,0},{2,1},{3,2},{5,4},{6,5},{7,6},{9,8},{10,9},{11,10},{13,12},{... | collective-permute-start | bytes 13832 | tf_op jit(solution)/shard_map/ppermute | solution.py:17
  28.5 7.1 %collective-permute-start.3 = (f32[64,18,1]{0,2,1:T(1,128)S(1)}, f32[64,18,1]{0,2,1:T(1,128)S(1)}, u32[]{:S(2)}, u32[]{:S(2)}) collective-permute-start(f32[64,18,1]{0,2,1:T(1,128)S(1)} %copy.45), channel_id=1, source_target_pairs={{0,1},{1,2},{2,3},{4,5},{5,6},{6,7},{8,9},{9,10},{10,11},{12,13},{... | collective-permute-start | bytes 13832 | tf_op jit(solution)/shard_map/ppermute | solution.py:14
  164.5 16.5 %collective-permute-start.5 = (f32[64,1,128]{2,0,1:T(8,128)S(1)}, f32[64,1,128]{2,0,1:T(8,128)S(1)}, u32[]{:S(2)}, u32[]{:S(2)}) collective-permute-start(f32[64,1,128]{2,0,1:T(8,128)S(1)} %get-tuple-element.19), channel_id=1, source_target_pairs={{0,4},{4,8},{8,12},{12,16},{16,20},{20,24},{24,28},{1,5},{5,9},{9,... | collective-permute-start | bytes 98312 | tf_op jit(solution)/shard_map/ppermute | solution.py:14
  179.6 3.8 collective-permute-start.4
  180.9 188.1 %reduce-scatter.11.cloned.1.call-start = ((), (), s32[]{:S(2)}) async-start(), calls=%async_computation.5 | async-start | bytes 294912 | tf_op jit(solution)/shard_map/reduce_scatter | solution.py:50
  183.8 6.1 %collective-permute-start.6 = (f32[64,18,1]{0,2,1:T(1,128)S(1)}, f32[64,18,1]{0,2,1:T(1,128)S(1)}, u32[]{:S(2)}, u32[]{:S(2)}) collective-permute-start(f32[64,18,1]{0,2,1:T(1,128)S(1)} %copy.60), channel_id=1, source_target_pairs={{1,0},{2,1},{3,2},{5,4},{6,5},{7,6},{9,8},{10,9},{11,10},{13,12},{... | collective-permute-start | bytes 13832 | tf_op jit(solution)/shard_map/ppermute | solution.py:17
  185.4 5.9 %collective-permute-start.7 = (f32[64,18,1]{0,2,1:T(1,128)S(1)}, f32[64,18,1]{0,2,1:T(1,128)S(1)}, u32[]{:S(2)}, u32[]{:S(2)}) collective-permute-start(f32[64,18,1]{0,2,1:T(1,128)S(1)} %copy.62), channel_id=1, source_target_pairs={{0,1},{1,2},{2,3},{4,5},{5,6},{6,7},{8,9},{9,10},{10,11},{12,13},{... | collective-permute-start | bytes 13832 | tf_op jit(solution)/shard_map/ppermute | solution.py:14
  316.9 16.6 %collective-permute-start.9 = (f32[64,1,128]{2,0,1:T(8,128)S(1)}, f32[64,1,128]{2,0,1:T(8,128)S(1)}, u32[]{:S(2)}, u32[]{:S(2)}) collective-permute-start(f32[64,1,128]{2,0,1:T(8,128)S(1)} %get-tuple-element.17), channel_id=1, source_target_pairs={{0,4},{4,8},{8,12},{12,16},{16,20},{20,24},{24,28},{1,5},{5,9},{9,... | collective-permute-start | bytes 98312 | tf_op jit(solution)/shard_map/ppermute | solution.py:14
  332.0 3.8 collective-permute-start.8
  336.3 7.0 %collective-permute-start.10 = (f32[64,18,1]{0,2,1:T(1,128)S(1)}, f32[64,18,1]{0,2,1:T(1,128)S(1)}, u32[]{:S(2)}, u32[]{:S(2)}) collective-permute-start(f32[64,18,1]{0,2,1:T(1,128)S(1)} %copy.78), channel_id=1, source_target_pairs={{1,0},{2,1},{3,2},{5,4},{6,5},{7,6},{9,8},{10,9},{11,10},{13,12},{... | collective-permute-start | bytes 13832 | tf_op jit(solution)/shard_map/ppermute | solution.py:17
  337.8 5.9 %collective-permute-start.11 = (f32[64,18,1]{0,2,1:T(1,128)S(1)}, f32[64,18,1]{0,2,1:T(1,128)S(1)}, u32[]{:S(2)}, u32[]{:S(2)}) collective-permute-start(f32[64,18,1]{0,2,1:T(1,128)S(1)} %copy.80), channel_id=1, source_target_pairs={{0,1},{1,2},{2,3},{4,5},{5,6},{6,7},{8,9},{9,10},{10,11},{12,13},{... | collective-permute-start | bytes 13832 | tf_op jit(solution)/shard_map/ppermute | solution.py:14
Sparse Core Ops, SparseCore 0:
  26.5 37.0 reduce-scatter.6
  181.0 35.2 reduce-scatter.8
  333.6 35.2 reduce-scatter.10
where the time goes:
time: 473 us; the launch traced here: 464 us
  blocking collectives  231 us (49%)
  waiting for transfers between devices  83.4 us (18%)
  matrix products  70.9 us (15%)
  starting transfers between devices  30.3 us (6%)
  other arithmetic  26.2 us (6%)
  between operations  15.1 us (3%)
  local copies, waits for them, and re-layouts  6.75 us (1%)
    psum x6, blocking collectives, total_terms(): summed = lax.psum((shares[0],), 'lon')  106 us
    reduce_scatter x3, waiting for transfers between devices, total_terms(): lax.psum_scatter(term_tuple[0], 'lat', scatter_dimension=0, tiled=True)  77.4 us
    unnamed x3, blocking collectives  70.8 us
    all_gather x6, blocking collectives, total_terms(): return (lax.all_gather(summed[0], 'lat', axis=0, tiled=True),)  54.5 us
    dot_general x3, matrix products, project_points(): jnp.einsum('tab,kab->tk', snapshots, masked_field, precision=lax.Precisio...  38.5 us
    dot_general x3, matrix products, expand_points(): jnp.einsum('tab,tk->kab', snapshots, coeffs, precision=lax.Precision.HIGH...  29.4 us
    ppermute x6, starting transfers between devices, padded_2(): lax.ppermute(lax.slice_in_dim(block, block.shape[dim] - width, None, axis...  22.2 us
    another operation x6, other arithmetic, local(): factor = jnp.linalg.cholesky(moments / point_count)  13 us
  transfers between devices with their start and end apart: 15, of which 7 were waited for; matrix products, arithmetic and copies ran while one was open for 9% of the time, Pallas kernels for 0%

commit v1 on v0

--- a/solution.py
+++ b/solution.py
@@ -47,9 +47,34 @@
 
 
 def total_terms(term_tuple):
+
+    def _resolve_trees(payload):
+        p_next, local_now, tile_out = (lax.psum(1, "lat"), lax.axis_index("lat"), payload.shape[0])
+        lanes = tuple(((to_i, (to_i + 1) % p_next) for to_i in range(p_next)))
+        oldest = jnp.zeros(
+            (*payload.shape[:0], p_next * tile_out, *payload.shape[1:]), payload.dtype
+        )
+        fields = tuple(((to_i, (to_i - 1) % p_next) for to_i in range(p_next)))
+        oldest = lax.dynamic_update_slice_in_dim(oldest, payload, local_now * tile_out, axis=0)
+        tall = g_now = payload
+        j = 1
+        right_arr = p_next // 2
+        while j < right_arr + 1:
+            tall = lax.ppermute(tall, "lat", lanes)
+            oldest = lax.dynamic_update_slice_in_dim(
+                oldest, tall, (local_now - j) % p_next * tile_out, axis=0
+            )
+            if j < p_next - right_arr:
+                g_now = lax.ppermute(g_now, "lat", fields)
+                oldest = lax.dynamic_update_slice_in_dim(
+                    oldest, g_now, (local_now + j) % p_next * tile_out, axis=0
+                )
+            j += 1
+        return oldest
+
     shares = (lax.psum_scatter(term_tuple[0], "lat", scatter_dimension=0, tiled=True),)
     summed = lax.psum((shares[0],), "lon")
-    return (lax.all_gather(summed[0], "lat", axis=0, tiled=True),)
+    return (_resolve_trees(summed[0]),)
 
 
 def local(snapshots, land_sea, penalty, initial_basis):

time: 473 us -> 512 us (1.082)
  blocking collectives: 231 us -> 173 us
  starting transfers between devices: 30.3 us -> 77 us
  waiting for transfers between devices: 83.4 us -> 123 us
  local copies, waits for them, and re-layouts: 6.75 us -> 16.6 us
    all_gather x6 -> x0, blocking collectives: 54.5 us -> none  [total_terms(): return (lax.all_gather(summed[0], 'lat', axis=0, tiled=True),)]
    ppermute x0 -> x42, starting transfers between devices: none -> 48.6 us  [the longest x18 47.6 us: _resolve_trees(): g_now = lax.ppermute(g_now, 'lat', fields)]
    ppermute x0 -> x42, waiting for transfers between devices: none -> 43.8 us  [the longest x24 43.7 us: _resolve_trees(): tall = lax.ppermute(tall, 'lat', lanes)]
    dynamic_update_slice x0 -> x48, local copies, waits for them, and re-layouts: none -> 10.2 us  [the longest x24 5.27 us: _resolve_trees(): lax.dynamic_update_slice_in_dim(oldest, tall, (local_now - j) % p_next *...]
  transfers between devices with their start and end apart: 15 -> 57, of which waited for: 7 -> 31; matrix products, arithmetic and copies ran while one was open for 9% -> 10% of each run, Pallas kernels for 0% -> 0%
where the time goes in v1:
time: 512 us; the launch traced here: 503 us
  blocking collectives  173 us (34%)
  waiting for transfers between devices  123 us (24%)
  starting transfers between devices  77 us (15%)
  matrix products  70.9 us (14%)
  other arithmetic  26.1 us (5%)
  local copies, waits for them, and re-layouts  16.6 us (3%)
  between operations  15.8 us (3%)
    psum x6, blocking collectives, total_terms(): summed = lax.psum((shares[0],), 'lon')  106 us
    reduce_scatter x3, waiting for transfers between devices, total_terms(): lax.psum_scatter(term_tuple[0], 'lat', scatter_dimension=0, tiled=True)  73.7 us
    unnamed x3, blocking collectives  67.1 us
    ppermute x18, starting transfers between devices, _resolve_trees(): g_now = lax.ppermute(g_now, 'lat', fields)  47.6 us
    ppermute x24, waiting for transfers between devices, _resolve_trees(): tall = lax.ppermute(tall, 'lat', lanes)  43.7 us
    dot_general x3, matrix products, project_points(): jnp.einsum('tab,kab->tk', snapshots, masked_field, precision=lax.Precisio...  38.5 us
    dot_general x3, matrix products, expand_points(): jnp.einsum('tab,tk->kab', snapshots, coeffs, precision=lax.Precision.HIGH...  29.5 us
    ppermute x6, starting transfers between devices, padded_2(): lax.ppermute(lax.slice_in_dim(block, block.shape[dim] - width, None, axis...  20.5 us
  transfers between devices with their start and end apart: 57, of which 31 were waited for; matrix products, arithmetic and copies ran while one was open for 10% of the time, Pallas kernels for 0%

profile of v1, /device:TPU:0, one launch (start us, length us, event | category | flops | bytes accessed | tf_op | source)
XLA Modules:
  0.0 502.9 jit_solution(12947546365785691878)
XLA Ops:
  10.5 3.0 collective-permute-start.8
  13.5 12.8 %fusion.39 = f32[1024,64]{0,1:T(8,128)} fusion(f32[64,16,128]{2,0,1:T(8,128)S(1)} %copy_multiply_fusion, f32[1024,16,128]{2,1,0:T(8,128)} %param.7), kind=kOutput, calls=%fused_computation.22 | convolution fusion | flops 1610612736 | bytes 9175040 | tf_op jit(solution)/shard_map/tab,kab->tk/dot_general | solution.py:31
  28.5 5.6 %collective-permute-start.10 = (f32[64,18,1]{0,2,1:T(1,128)S(1)}, f32[64,18,1]{0,2,1:T(1,128)S(1)}, u32[]{:S(2)}, u32[]{:S(2)}) collective-permute-start(f32[64,18,1]{0,2,1:T(1,128)S(1)} %copy.53), channel_id=1, source_target_pairs={{0,1},{1,2},{2,3},{4,5},{5,6},{6,7},{8,9},{9,10},{10,11},{12,13},{... | collective-permute-start | bytes 13832 | tf_op jit(solution)/shard_map/ppermute | solution.py:14
  36.0 27.6 %reduce-scatter.7.cloned.1.call-done = f32[128,64]{0,1:T(8,128)} async-done(((f32[1024,64]{0,1:T(8,128)}), f32[128,64]{0,1:T(8,128)}) %reduce-scatter.7.cloned.1.call-update) | async-done | bytes 32784 | tf_op jit(solution)/shard_map/reduce_scatter | solution.py:75
  63.6 19.6 %psum.42 = f32[128,64]{0,1:T(8,128)S(1)} all-reduce(f32[128,64]{0,1:T(8,128)} %reduce-scatter.7.cloned.1.call-done), channel_id=1, replica_groups=mesh['lat'=8,'lon'=4] {'lon'}, use_global_device_ids=true, to_apply=%region_1.0 | all-reduce | flops 8192 | bytes 65536 | tf_op jit(solution)/shard_map/psum | solution.py:76
  83.3 2.6 collective-permute-start.1
  86.0 1.6 collective-permute-done
  87.5 2.6 collective-permute-start.3
  90.2 1.7 collective-permute-done.2
  91.9 2.6 collective-permute-start.5
  94.5 1.6 collective-permute-done.4
  96.1 4.2 collective-permute-done.6
  100.4 9.8 %fusion.36 = f32[64,16,128]{2,0,1:T(8,128)S(1)} fusion(f32[1024,16,128]{2,1,0:T(8,128)} %param.7, f32[64,18,1]{2,0,1:T(8,128)S(1)} %copy.54, f32[64,1,128]{2,0,1:T(8,128)S(1)} %collective-permute-done.7, f32[64,16,128]{2,0,1:T(8,128)S(1)} %copy_multiply_fusion, f32[64,1,128]{2,0,1:T(8,128)S(1)} %collective-permute-done.8, f32[64,18,1]{2,0,1:T(8,128)S(1)} %copy.52, ...), kind=kOutput, calls=%fused_computation.20 | convolution fusion | flops 1612840960 | bytes 9790464 | tf_op jit(solution)/shard_map/tab,tk->kab/dot_general | solution.py:35
  110.7 22.4 %all-reduce = f32[64,64]{0,1:T(8,128)S(1)} all-reduce(f32[64,64]{0,1:T(8,128)S(1)} %convolution_bitcast_fusion.3), channel_id=3, replica_groups=mesh['lat'=8,'lon'=4] {'lat'}, use_global_device_ids=true, to_apply=%region_2.3.clone | all-reduce | flops 4096 | bytes 32768
  133.2 15.8 %psum.43 = f32[8,64]{0,1:T(8,128)S(1)} all-reduce(f32[8,64]{0,1:T(8,128)S(1)} %constant_dynamic-slice_fusion.2), channel_id=1, replica_groups=mesh['lat'=8,'lon'=4] {'lon'}, use_global_device_ids=true, to_apply=%region_3.4 | all-reduce | flops 512 | bytes 4096 | tf_op jit(solution)/shard_map/psum | solution.py:76
  149.0 2.6 collective-permute-start.12
  151.6 1.6 collective-permute-done.11
  153.2 2.6 collective-permute-start.14
  155.9 1.6 collective-permute-done.13
  157.5 2.6 collective-permute-start.16
  160.1 1.6 collective-permute-done.15
  166.9 5.8 %cholesky.44 = f32[64,64]{1,0:T(8,128)S(1)} custom-call(f32[64,64]{1,0:T(8,128)S(1)} %fusion.76), custom_call_target="Cholesky" | custom-call | tf_op jit(solution)/shard_map/jit(cholesky)/cholesky | solution.py:92
  174.1 4.9 custom-call.6
  181.0 12.8 %fusion.42 = f32[1024,64]{0,1:T(8,128)} fusion(f32[1024,16,128]{2,1,0:T(8,128)} %param.7, f32[8,16,8,128]{3,2,1,0:T(8,128)S(1)} %convolution_bitcast_fusion), kind=kOutput, calls=%fused_computation.23 | convolution fusion | flops 1610612736 | bytes 9175040 | tf_op jit(solution)/shard_map/tab,kab->tk/dot_general | solution.py:31
  195.3 1.7 collective-permute-done.25
  199.0 4.6 collective-permute-start.28
  205.1 23.0 %reduce-scatter.9.cloned.1.call-done = f32[128,64]{0,1:T(8,128)} async-done(((f32[1024,64]{0,1:T(8,128)}), f32[128,64]{0,1:T(8,128)}) %reduce-scatter.9.cloned.1.call-update) | async-done | bytes 32784 | tf_op jit(solution)/shard_map/reduce_scatter | solution.py:75
  228.2 19.6 %psum.44 = f32[128,64]{0,1:T(8,128)S(1)} all-reduce(f32[128,64]{0,1:T(8,128)} %reduce-scatter.9.cloned.1.call-done), channel_id=1, replica_groups=mesh['lat'=8,'lon'=4] {'lon'}, use_global_device_ids=true, to_apply=%region_7.10 | all-reduce | flops 8192 | bytes 65536 | tf_op jit(solution)/shard_map/psum | solution.py:76
  247.9 2.6 collective-permute-start.19
  250.5 1.6 collective-permute-done.18
  252.1 2.7 collective-permute-start.21
  254.8 1.6 collective-permute-done.20
  256.4 2.7 collective-permute-start.23
  260.9 4.2 collective-permute-done.24
  265.0 9.8 %fusion.33 = f32[64,16,128]{2,0,1:T(8,128)S(1)} fusion(f32[1024,16,128]{2,1,0:T(8,128)} %param.7, f32[64,18,128]{2,0,1:T(8,128)S(1)} %constant_dynamic-update-slice_fusion, f32[64,18,1]{2,0,1:T(8,128)S(1)} %copy.69, f32[64,18,1]{2,0,1:T(8,128)S(1)} %copy.67, f32[64,16,128]{2,0,1:T(8,128)S(1)} %bitcast.101, f32[64,1,128]{2,0,1:T(8,128)S(1)} %collective-permute-done.26, ...), kind=kOutput, calls=%fused_computation.19 | convolution fusion | flops 1612316672 | bytes 10380288 | tf_op jit(solution)/shard_map/tab,tk->kab/dot_general | solution.py:35
  275.4 22.4 %all-reduce.1 = f32[64,64]{0,1:T(8,128)S(1)} all-reduce(f32[64,64]{0,1:T(8,128)S(1)} %convolution_bitcast_fusion.2), channel_id=5, replica_groups=mesh['lat'=8,'lon'=4] {'lat'}, use_global_device_ids=true, to_apply=%region_8.11.clone | all-reduce | flops 4096 | bytes 32768
  297.9 15.8 %psum.45 = f32[8,64]{0,1:T(8,128)S(1)} all-reduce(f32[8,64]{0,1:T(8,128)S(1)} %constant_dynamic-slice_fusion.1), channel_id=1, replica_groups=mesh['lat'=8,'lon'=4] {'lon'}, use_global_device_ids=true, to_apply=%region_9.12 | all-reduce | flops 512 | bytes 4096 | tf_op jit(solution)/shard_map/psum | solution.py:76
  313.7 2.6 collective-permute-start.30
  316.3 1.6 collective-permute-done.29
  317.9 2.6 collective-permute-start.32
  320.6 1.6 collective-permute-done.31
  322.2 2.6 collective-permute-start.34
  324.8 1.6 collective-permute-done.33
  331.2 5.8 %cholesky.55 = f32[64,64]{1,0:T(8,128)S(1)} custom-call(f32[64,64]{1,0:T(8,128)S(1)} %fusion.74), custom_call_target="Cholesky" | custom-call | tf_op jit(solution)/shard_map/jit(cholesky)/cholesky | solution.py:92
  338.3 4.9 custom-call.7
  345.5 12.8 %fusion.45 = f32[1024,64]{0,1:T(8,128)} fusion(f32[1024,16,128]{2,1,0:T(8,128)} %param.7, f32[64,2048]{1,0:T(8,128)S(1)} %fusion.48), kind=kOutput, calls=%fused_computation.24 | convolution fusion | flops 1610612736 | bytes 9175040 | tf_op jit(solution)/shard_map/tab,kab->tk/dot_general | solution.py:31
  359.7 1.7 collective-permute-done.43
  363.4 4.6 collective-permute-start.46
  369.6 23.1 %reduce-scatter.11.cloned.1.call-done = f32[128,64]{0,1:T(8,128)} async-done(((f32[1024,64]{0,1:T(8,128)}), f32[128,64]{0,1:T(8,128)}) %reduce-scatter.11.cloned.1.call-update) | async-done | bytes 32784 | tf_op jit(solution)/shard_map/reduce_scatter | solution.py:75
  392.7 19.6 %psum.46 = f32[128,64]{0,1:T(8,128)S(1)} all-reduce(f32[128,64]{0,1:T(8,128)} %reduce-scatter.11.cloned.1.call-done), channel_id=1, replica_groups=mesh['lat'=8,'lon'=4] {'lon'}, use_global_device_ids=true, to_apply=%region_11.14 | all-reduce | flops 8192 | bytes 65536 | tf_op jit(solution)/shard_map/psum | solution.py:76
  412.4 2.6 collective-permute-start.37
  416.6 2.7 collective-permute-start.39
  419.3 1.6 collective-permute-done.38
  421.0 2.7 collective-permute-start.41
  425.3 4.2 collective-permute-done.42
  429.4 9.8 %fusion.30 = f32[64,16,128]{2,0,1:T(8,128)S(1)} fusion(f32[1024,16,128]{2,1,0:T(8,128)} %param.7, f32[64,18,128]{2,0,1:T(8,128)S(1)} %constant_dynamic-update-slice_fusion.3, f32[64,18,1]{2,0,1:T(8,128)S(1)} %copy.85, f32[64,18,1]{2,0,1:T(8,128)S(1)} %copy.83, f32[64,16,128]{2,0,1:T(8,128)S(1)} %copy_bitcast_fusion, ...), kind=kOutput, calls=%fused_computation.18 | convolution fusion | flops 1612316672 | bytes 10380288 | tf_op jit(solution)/shard_map/tab,tk->kab/dot_general | solution.py:35
  439.9 22.4 %all-reduce.2 = f32[64,64]{0,1:T(8,128)S(1)} all-reduce(f32[64,64]{0,1:T(8,128)S(1)} %convolution_bitcast_fusion.1), channel_id=7, replica_groups=mesh['lat'=8,'lon'=4] {'lat'}, use_global_device_ids=true, to_apply=%region_12.15.clone | all-reduce | flops 4096 | bytes 32768
  462.3 15.8 %psum.47 = f32[8,64]{0,1:T(8,128)S(1)} all-reduce(f32[8,64]{0,1:T(8,128)S(1)} %constant_dynamic-slice_fusion), channel_id=1, replica_groups=mesh['lat'=8,'lon'=4] {'lon'}, use_global_device_ids=true, to_apply=%region_13.16 | all-reduce | flops 512 | bytes 4096 | tf_op jit(solution)/shard_map/psum | solution.py:76
  478.1 2.6 collective-permute-start.48
  480.8 1.6 collective-permute-done.47
  482.4 2.6 collective-permute-start.50
  485.0 1.6 collective-permute-done.49
  486.6 2.6 collective-permute-start.52
  489.2 1.6 collective-permute-done.51
  (183 shorter events, 45.5 us)
Async XLA Ops:
  7.2 27.0 %copy-start.1 = (u32[32]{0:T(128)S(1)}, u32[32]{0:T(128)}, u32[]{:S(2)}) copy-start(u32[32]{0:T(128)} %constant.182) | copy-start | bytes 388
  7.2 56.4 %reduce-scatter.7.cloned.1.call-start = ((), (), s32[]{:S(2)}) async-start(), calls=%async_computation.3 | async-start | bytes 294912 | tf_op jit(solution)/shard_map/reduce_scatter | solution.py:75
  9.1 91.2 %copy-start = (f32[16,128]{1,0:T(8,128)S(1)}, f32[16,128]{1,0:T(8,128)}, u32[]{:S(2)}) copy-start(f32[16,128]{1,0:T(8,128)} %param.9) | copy-start | bytes 24580
  9.2 17.3 %collective-permute-start.7 = (f32[64,1,128]{2,0,1:T(8,128)S(1)}, f32[64,1,128]{2,0,1:T(8,128)S(1)}, u32[]{:S(2)}, u32[]{:S(2)}) collective-permute-start(f32[64,1,128]{2,0,1:T(8,128)S(1)} %get-tuple-element.21), channel_id=1, source_target_pairs={{4,0},{8,4},{12,8},{16,12},{20,16},{24,20},{28,24},{5,1},{9,5},{13... | collective-permute-start | bytes 98312 | tf_op jit(solution)/shard_map/ppermute | solution.py:17
  10.5 16.0 %collective-permute-start.8 = (f32[64,1,128]{2,0,1:T(8,128)S(1)}, f32[64,1,128]{2,0,1:T(8,128)S(1)}, u32[]{:S(2)}, u32[]{:S(2)}) collective-permute-start(f32[64,1,128]{2,0,1:T(8,128)S(1)} %get-tuple-element.20), channel_id=1, source_target_pairs={{0,4},{4,8},{8,12},{12,16},{16,20},{20,24},{24,28},{1,5},{5,9},{9,... | collective-permute-start | bytes 98312 | tf_op jit(solution)/shard_map/ppermute | solution.py:14
  26.4 201.8 %reduce-scatter.9.cloned.1.call-start = ((), (), s32[]{:S(2)}) async-start(), calls=%async_computation.4 | async-start | bytes 294912 | tf_op jit(solution)/shard_map/reduce_scatter | solution.py:75
  27.0 8.5 %collective-permute-start.9 = (f32[64,18,1]{0,2,1:T(1,128)S(1)}, f32[64,18,1]{0,2,1:T(1,128)S(1)}, u32[]{:S(2)}, u32[]{:S(2)}) collective-permute-start(f32[64,18,1]{0,2,1:T(1,128)S(1)} %copy.51), channel_id=1, source_target_pairs={{1,0},{2,1},{3,2},{5,4},{6,5},{7,6},{9,8},{10,9},{11,10},{13,12},{... | collective-permute-start | bytes 13832 | tf_op jit(solution)/shard_map/ppermute | solution.py:17
  28.5 7.2 %collective-permute-start.10 = (f32[64,18,1]{0,2,1:T(1,128)S(1)}, f32[64,18,1]{0,2,1:T(1,128)S(1)}, u32[]{:S(2)}, u32[]{:S(2)}) collective-permute-start(f32[64,18,1]{0,2,1:T(1,128)S(1)} %copy.53), channel_id=1, source_target_pairs={{0,1},{1,2},{2,3},{4,5},{5,6},{6,7},{8,9},{9,10},{10,11},{12,13},{... | collective-permute-start | bytes 13832 | tf_op jit(solution)/shard_map/ppermute | solution.py:14
  83.2 4.3 collective-permute-start
  83.3 4.2 collective-permute-start.1
  87.5 4.4 collective-permute-start.2
  87.5 4.4 collective-permute-start.3
  91.9 4.2 collective-permute-start.4
  91.9 4.2 collective-permute-start.5
  96.1 4.2 collective-permute-start.6
  148.9 4.3 collective-permute-start.11
  149.0 4.2 collective-permute-start.12
  153.2 4.2 collective-permute-start.13
  153.2 4.2 collective-permute-start.14
  157.4 4.2 collective-permute-start.15
  157.5 7.4 %collective-permute-start.16 = (f32[8,64]{0,1:T(8,128)S(1)}, f32[8,64]{0,1:T(8,128)S(1)}, u32[]{:S(2)}, u32[]{:S(2)}) collective-permute-start(f32[8,64]{0,1:T(8,128)S(1)} %collective-permute-done.14), channel_id=1, source_target_pairs={{0,28},{4,0},{8,4},{12,8},{16,12},{20,16},{24,20},{28,24},{1,29},{... | collective-permute-start | bytes 6152 | tf_op jit(solution)/shard_map/ppermute | solution.py:68
  161.7 4.7 collective-permute-start.17
  179.7 15.5 %collective-permute-start.26 = (f32[64,1,128]{2,0,1:T(8,128)S(1)}, f32[64,1,128]{2,0,1:T(8,128)S(1)}, u32[]{:S(2)}, u32[]{:S(2)}) collective-permute-start(f32[64,1,128]{2,0,1:T(8,128)S(1)} %get-tuple-element.19), channel_id=1, source_target_pairs={{0,4},{4,8},{8,12},{12,16},{16,20},{20,24},{24,28},{1,5},{5,9},{9,... | collective-permute-start | bytes 98312 | tf_op jit(solution)/shard_map/ppermute | solution.py:14
  193.8 198.9 %reduce-scatter.11.cloned.1.call-start = ((), (), s32[]{:S(2)}) async-start(), calls=%async_computation.5 | async-start | bytes 294912 | tf_op jit(solution)/shard_map/reduce_scatter | solution.py:75
  193.9 3.1 collective-permute-start.25
  197.4 6.1 %collective-permute-start.27 = (f32[64,18,1]{0,2,1:T(1,128)S(1)}, f32[64,18,1]{0,2,1:T(1,128)S(1)}, u32[]{:S(2)}, u32[]{:S(2)}) collective-permute-start(f32[64,18,1]{0,2,1:T(1,128)S(1)} %copy.66), channel_id=1, source_target_pairs={{1,0},{2,1},{3,2},{5,4},{6,5},{7,6},{9,8},{10,9},{11,10},{13,12},{... | collective-permute-start | bytes 13832 | tf_op jit(solution)/shard_map/ppermute | solution.py:17
  199.0 5.9 %collective-permute-start.28 = (f32[64,18,1]{0,2,1:T(1,128)S(1)}, f32[64,18,1]{0,2,1:T(1,128)S(1)}, u32[]{:S(2)}, u32[]{:S(2)}) collective-permute-start(f32[64,18,1]{0,2,1:T(1,128)S(1)} %copy.68), channel_id=1, source_target_pairs={{0,1},{1,2},{2,3},{4,5},{5,6},{6,7},{8,9},{9,10},{10,11},{12,13},{... | collective-permute-start | bytes 13832 | tf_op jit(solution)/shard_map/ppermute | solution.py:14
  247.8 4.3 collective-permute-start.18
  247.9 4.2 collective-permute-start.19
  252.1 4.3 collective-permute-start.20
  252.1 4.3 collective-permute-start.21
  256.4 4.2 collective-permute-start.22
  256.4 4.4 collective-permute-start.23
  260.7 4.4 collective-permute-start.24
  313.6 4.3 collective-permute-start.29
  313.7 4.2 collective-permute-start.30
  317.9 4.2 collective-permute-start.31
  317.9 4.2 collective-permute-start.32
  322.2 4.2 collective-permute-start.33
  322.2 6.8 %collective-permute-start.34 = (f32[8,64]{0,1:T(8,128)S(1)}, f32[8,64]{0,1:T(8,128)S(1)}, u32[]{:S(2)}, u32[]{:S(2)}) collective-permute-start(f32[8,64]{0,1:T(8,128)S(1)} %collective-permute-done.32), channel_id=1, source_target_pairs={{0,28},{4,0},{8,4},{12,8},{16,12},{20,16},{24,20},{28,24},{1,29},{... | collective-permute-start | bytes 6152 | tf_op jit(solution)/shard_map/ppermute | solution.py:68
  326.4 4.2 collective-permute-start.35
  344.0 15.7 %collective-permute-start.44 = (f32[64,1,128]{2,0,1:T(8,128)S(1)}, f32[64,1,128]{2,0,1:T(8,128)S(1)}, u32[]{:S(2)}, u32[]{:S(2)}) collective-permute-start(f32[64,1,128]{2,0,1:T(8,128)S(1)} %get-tuple-element.17), channel_id=1, source_target_pairs={{0,4},{4,8},{8,12},{12,16},{16,20},{20,24},{24,28},{1,5},{5,9},{9,... | collective-permute-start | bytes 98312 | tf_op jit(solution)/shard_map/ppermute | solution.py:14
  358.3 3.1 collective-permute-start.43
  361.9 6.1 %collective-permute-start.45 = (f32[64,18,1]{0,2,1:T(1,128)S(1)}, f32[64,18,1]{0,2,1:T(1,128)S(1)}, u32[]{:S(2)}, u32[]{:S(2)}) collective-permute-start(f32[64,18,1]{0,2,1:T(1,128)S(1)} %copy.82), channel_id=1, source_target_pairs={{1,0},{2,1},{3,2},{5,4},{6,5},{7,6},{9,8},{10,9},{11,10},{13,12},{... | collective-permute-start | bytes 13832 | tf_op jit(solution)/shard_map/ppermute | solution.py:17
  363.4 5.9 %collective-permute-start.46 = (f32[64,18,1]{0,2,1:T(1,128)S(1)}, f32[64,18,1]{0,2,1:T(1,128)S(1)}, u32[]{:S(2)}, u32[]{:S(2)}) collective-permute-start(f32[64,18,1]{0,2,1:T(1,128)S(1)} %copy.84), channel_id=1, source_target_pairs={{0,1},{1,2},{2,3},{4,5},{5,6},{6,7},{8,9},{9,10},{10,11},{12,13},{... | collective-permute-start | bytes 13832 | tf_op jit(solution)/shard_map/ppermute | solution.py:14
  412.3 4.3 collective-permute-start.36
  412.4 4.2 collective-permute-start.37
  416.6 4.3 collective-permute-start.38
  416.6 4.3 collective-permute-start.39
  421.0 4.2 collective-permute-start.40
  421.0 4.3 collective-permute-start.41
  425.2 4.2 collective-permute-start.42
  478.1 4.3 collective-permute-start.47
  478.1 4.2 collective-permute-start.48
  482.4 4.2 collective-permute-start.49
  482.4 4.2 collective-permute-start.50
  486.6 4.2 collective-permute-start.51
  486.6 7.7 %collective-permute-start.52 = (f32[8,64]{0,1:T(8,128)S(1)}, f32[8,64]{0,1:T(8,128)S(1)}, u32[]{:S(2)}, u32[]{:S(2)}) collective-permute-start(f32[8,64]{0,1:T(8,128)S(1)} %collective-permute-done.50), channel_id=1, source_target_pairs={{0,28},{4,0},{8,4},{12,8},{16,12},{20,16},{24,20},{28,24},{1,29},{... | collective-permute-start | bytes 6152 | tf_op jit(solution)/shard_map/ppermute | solution.py:68
  490.8 4.2 collective-permute-start.53
Sparse Core Ops, SparseCore 0:
  26.5 37.0 reduce-scatter.6
  194.0 34.1 reduce-scatter.8
  358.4 34.2 reduce-scatter.10
